TPU v7x, 512 devices: a whole 4x8x8 slice. The times are simulated.
512 devices in a mesh: grp: 64 (over z, y), row: 8 (over x, core).
Axes of the slice: x: 4, y: 8, z: 8, core: 2. Of those that a mesh axis runs over, the one named last changes fastest.
Arguments:
- latents: bfloat16 [64, 16384], P('grp'), may hold values from -6 to 6
- frames: int32 [64], replicated, may hold values from 1 to 4, as said below
- offsets: int32 [64], replicated, may hold values from 0 to 1008, as said below
- assign: int32 [64], replicated, may hold values from 0 to 63, each once
- w_in: bfloat16 [16, 27, 384], replicated, may hold values from -0.3125 to 0.3125
- w_mid: bfloat16 [384, 27, 192], P('grp'), may hold values from -0.0625 to 0.0625
- w_out: bfloat16 [192, 27, 96], P('grp'), may hold values from -0.078125 to 0.078125
- gain_in: float32 [384], replicated, may hold values from 0.25 to 1.75
- gain_mid: float32 [192], replicated, may hold values from 0.25 to 1.75
- gain_out: float32 [96], replicated, may hold values from 0.25 to 1.75
Outputs:
- decoded: bfloat16 [64, 4, 64, 6144], P('grp', None, 'row')
Inputs may be any that keep to these rules, and one draw needn't show every extreme that they name: Some request has exactly 4 frames. The blocks of different requests do not intersect, and offsets[r] + 16 <= 1024 for every request; some request starts at 1008. `assign`: every request is decoded by exactly one group.
All inputs are finite; a program needn't handle non-finite values.
Results may differ from a plain program's by a relative error of at most 0.006.
Values may be sent and summed in bfloat16 or wider, within the bound.
A program may use at most 128 MiB of HBM per device.

v0:
```python
import jax
import jax.numpy as jnp
from jax import lax
from jax.sharding import PartitionSpec as P

RL = 2
WL = 16
FMAX = 4


def extended_2(cells, sides, width):
    for axis, dim in sides:
        count = lax.axis_size(axis)
        ends = count - 1
        head = lax.slice_in_dim(cells, 0, width, axis=dim)
        tail = lax.slice_in_dim(cells, cells.shape[dim] - width, cells.shape[dim], axis=dim)
        cells = jnp.concatenate(
            [
                lax.ppermute(tail, axis, [(i, (i + 1) % count) for i in range(ends)]),
                cells,
                lax.ppermute(head, axis, [((i + 1) % count, i) for i in range(ends)]),
            ],
            axis=dim,
        )
    return cells


def rms_silu(hidden, gain):
    mean_sq = jnp.mean(hidden * hidden, axis=-1, keepdims=True)
    scaled = hidden * lax.rsqrt(mean_sq + 1e-06) * gain
    return jax.nn.silu(scaled)


def causal_conv(extended, weight):
    count_t = extended.shape[0]
    count_r = extended.shape[1] - 2
    count_c = extended.shape[2]
    width_in = extended.shape[3]
    width_out = weight.shape[2]
    padded = jnp.pad(extended, ((2, 0), (0, 0), (1, 1), (0, 0)))
    total = jnp.zeros((count_t * count_r * count_c, width_out), jnp.float32)
    for time_tap in range(3):
        for row_tap in range(3):
            for col_tap in range(3):
                window = padded[
                    time_tap : time_tap + count_t,
                    row_tap : row_tap + count_r,
                    col_tap : col_tap + count_c,
                ]
                window = window.reshape(count_t * count_r * count_c, width_in)
                tap_index = 9 * time_tap + 3 * row_tap + col_tap
                total = total + jnp.dot(
                    window, weight[:, tap_index, :], preferred_element_type=jnp.float32
                )
    return total.reshape(count_t, count_r, count_c, width_out)


def upsample(values):
    return jnp.repeat(jnp.repeat(values, 2, axis=1), 2, axis=2)


def per_device(latents, frames, offsets, assign, w_in, w_mid, w_out, gain_in, gain_mid, gain_out):
    groups = lax.axis_size("grp")
    row_count = lax.axis_size("row")
    row_index = lax.axis_index("row")
    group_index = lax.axis_index("grp")
    channels = w_in.shape[0]
    cap_vals = latents.shape[1] // groups
    cap_tokens = cap_vals // channels
    span_len = cap_tokens // FMAX
    flat = latents[0]
    slot_ids = jnp.arange(cap_vals, dtype=jnp.int32)

    def select_span(request):
        start = offsets[request] * channels
        block = lax.dynamic_slice_in_dim(flat, start, cap_vals)
        keep = slot_ids < frames[request] * span_len * channels
        return jnp.where(keep, block, jnp.zeros((), block.dtype))

    outgoing = jax.vmap(select_span)(assign)
    incoming = lax.all_to_all(outgoing, "grp", split_axis=0, concat_axis=0, tiled=True)
    table = incoming.reshape(groups * cap_tokens, channels)
    request = assign[group_index]
    count = frames[request]
    fill_len = count * span_len
    image_rows = RL * row_count
    frame_ids = jnp.arange(FMAX, dtype=jnp.int32)[:, None, None]
    row_ids = row_index * RL + jnp.arange(RL, dtype=jnp.int32)[None, :, None]
    col_ids = jnp.arange(WL, dtype=jnp.int32)[None, None, :]
    position = (frame_ids * image_rows + row_ids) * WL + col_ids
    shard = jnp.minimum(position // fill_len, groups - 1)
    within = position % fill_len
    tokens = table[shard * cap_tokens + within]
    valid = (frame_ids < count)[..., None]
    latent_in = jnp.where(valid, tokens, jnp.zeros((), tokens.dtype))
    full_mid, full_out = (
        lax.all_gather(w_mid, "grp", axis=0, tiled=True),
        lax.all_gather(w_out, "grp", axis=0, tiled=True),
    )
    latent_ext = extended_2(latent_in, (("row", 1),), 1)
    act_in = rms_silu(causal_conv(latent_ext, w_in), gain_in).astype(jnp.bfloat16)
    mid_ext = extended_2(upsample(act_in), (("row", 1),), 1)
    act_mid = rms_silu(causal_conv(mid_ext, full_mid), gain_mid).astype(jnp.bfloat16)
    out_ext = extended_2(upsample(act_mid), (("row", 1),), 1)
    final = rms_silu(causal_conv(out_ext, full_out), gain_out)
    final = jnp.where(valid, final, jnp.zeros((), jnp.float32)).astype(jnp.bfloat16)
    return final.reshape(1, FMAX, 4 * RL, 4 * WL * final.shape[3])


def solution(mesh):
    placed = (
        P("grp", None),
        P(),
        P(),
        P(),
        P(),
        P("grp", None, None),
        P("grp", None, None),
        P(),
        P(),
        P(),
    )
    return jax.shard_map(
        per_device,
        mesh=mesh,
        in_specs=placed,
        out_specs=P("grp", None, "row", None),
        check_vma=False,
    )
```

profile of v0, /device:TPU:1, one launch (start us, length us, event | category | flops | bytes accessed | tf_op | source)
XLA Modules:
  0.0 352.4 jit_solution(12229377863620362657)
XLA Ops:
  8.7 1.4 gather_fusion
  11.2 94.7 %while.1 = (s32[]{:T(128)}, bf16[16384]{0:T(1024)(128)(2,1)S(1)}, s32[64,1]{0,1:T(1,128)S(1)}, bf16[64,256]{1,0:T(8,128)(2,1)S(1)}, s32[]{:T(128)}, /*index=5*/s32[]{:T(128)}) while((s32[]{:T(128)}, bf16[16384]{0:T(1024)(128)(2,1)S(1)}, s32[64,1]{0,1:T(1,128)S(1)}, bf16[64,256]{1,0:T(8,128)(2,1)S(1)}, s32[]{:T(128)}, /*index=5*/s32[]{:T(128)}) %tuple.141), condition=%wide.while_cond, body=%wide.while_body.sunk | while | flops 2 | bytes 3169 | solution.py:76
  107.8 17.2 %all-to-all-start = ((bf16[64,2,128]{2,1,0:T(2,128)(2,1)}), bf16[64,2,128]{2,1,0:T(2,128)(2,1)S(1)}, u32[]{:S(2)}, u32[]{:S(2)}) async-start(bf16[64,2,128]{2,1,0:T(2,128)(2,1)} %reshape.702), calls=%async_computation | async-start | bytes 65536 | tf_op jit(solution)/shard_map/all_to_all | solution.py:81
  125.1 1.3 dynamic_slice.6
  128.5 1.3 dynamic_slice.7
  131.8 4.0 %all-to-all-done = bf16[64,2,128]{2,1,0:T(2,128)(2,1)S(1)} async-done(((bf16[64,2,128]{2,1,0:T(2,128)(2,1)}), bf16[64,2,128]{2,1,0:T(2,128)(2,1)S(1)}, u32[]{:S(2)}, u32[]{:S(2)}) %all-to-all-start) | async-done | bytes 32800 | tf_op jit(solution)/shard_map/all_to_all | solution.py:81
  137.1 5.1 %collective-permute-start = (bf16[4,1,16,16]{3,2,1,0:T(8,128)(2,1)S(1)}, bf16[4,1,16,16]{3,2,1,0:T(8,128)(2,1)S(1)}, u32[]{:S(2)}, u32[]{:S(2)}) collective-permute-start(bf16[4,1,16,16]{3,2,1,0:T(8,128)(2,1)S(1)} %get-tuple-element.157), channel_id=1, source_target_pairs={{0,1},{1,2},{2,3},{3,4},{4,5},{5,6},{6,7},{8,9},{9,10},{10,11},{11... | collective-permute-start | bytes 6152 | tf_op jit(solution)/shard_map/ppermute | solution.py:19
  142.2 1.9 collective-permute-start.1
  144.2 37.3 %all_gather.7 = bf16[192,27,96]{2,1,0:T(8,128)(2,1)S(1)} all-gather(bf16[3,27,96]{2,1,0:T(8,128)(2,1)S(1)} %copy-done.91), channel_id=1, replica_groups=mesh['grp'=64,'row'=8] {'grp'}, dimensions={0}, use_global_device_ids=true | all-gather | bytes 1010880 | tf_op jit(solution)/shard_map/all_gather | solution.py:98
  186.6 14.6 %collective-permute-start.2 = (bf16[4,1,32,384]{3,2,1,0:T(8,128)(2,1)S(1)}, bf16[4,1,32,384]{3,2,1,0:T(8,128)(2,1)S(1)}, u32[]{:S(2)}, u32[]{:S(2)}) collective-permute-start(bf16[4,1,32,384]{3,2,1,0:T(8,128)(2,1)S(1)} %get-tuple-element.129), channel_id=1, source_target_pairs={{0,1},{1,2},{2,3},{3,4},{4,5},{5,6},{6,7},{8,9},{9,10},{10,11},{11... | collective-permute-start | bytes 294920 | tf_op jit(solution)/shard_map/ppermute | solution.py:19
  201.2 2.4 collective-permute-start.3
  203.6 2.8 fusion.132
  208.7 1.4 fusion.135
  210.1 3.3 fusion.134
  213.5 8.5 %fusion.129 = (bf16[384,1,192]{2,1,0:T(2,128)(2,1)}, bf16[384,1,192]{2,1,0:T(2,128)(2,1)}, bf16[384,1,192]{2,1,0:T(2,128)(2,1)}, bf16[384,1,192]{2,1,0:T(2,128)(...) fusion(bf16[384,27,192]{2,1,0:T(8,128)(2,1)} %all-gather.2.clon, ...), kind=kLoop, calls=%fused_computation.270 | loop fusion | bytes 2359296 | tf_op jit(solution)/shard_map/slice | solution.py:53
  222.0 1.8 copy.135
  223.8 1.8 copy.134
  225.6 1.8 copy.133
  227.4 1.2 copy.132
  233.2 16.4 %fusion.128 = (bf16[384,1,192]{2,1,0:T(2,128)(2,1)}, bf16[384,1,192]{2,1,0:T(2,128)(2,1)}, bf16[384,1,192]{2,1,0:T(2,128)(2,1)}, bf16[384,1,192]{2,1,0:T(2,128)(...) fusion(bf16[384,27,192]{2,1,0:T(8,128)(2,1)} %all-gather.2.clon, ...), kind=kLoop, calls=%fused_computation.269 | loop fusion | bytes 5603328 | tf_op jit(solution)/shard_map/slice | solution.py:53
  249.6 1.8 copy.154
  251.4 1.8 copy.153
  253.2 1.8 copy.152
  255.0 1.8 copy.151
  256.8 1.8 copy.150
  258.6 1.8 copy.149
  260.4 1.8 copy.148
  262.2 1.8 copy.147
  264.0 1.8 copy.146
  265.8 1.8 copy.145
  268.7 1.8 copy.143
  271.7 1.2 copy.141
  272.9 1.8 copy.140
  274.7 1.8 copy.139
  276.5 1.8 copy.138
  279.4 1.3 copy.136
  280.8 1.3 fusion.64
  282.1 1.3 fusion.36
  283.4 1.2 fusion.43
  293.7 1.8 broadcast_in_dim.66
  295.5 2.1 reshape.625
  298.3 3.6 %collective-permute-start.4 = (bf16[4,1,64,192]{3,2,1,0:T(8,128)(2,1)}, bf16[4,1,64,192]{3,2,1,0:T(8,128)(2,1)S(1)}, u32[]{:S(2)}, u32[]{:S(2)}) collective-permute-start(bf16[4,1,64,192]{3,2,1,0:T(8,128)(2,1)} %get-tuple-element.125), channel_id=1, source_target_pairs={{0,1},{1,2},{2,3},{3,4},{4,5},{5,6},{6,7},{8,9},{9,10},{10,11},{11... | collective-permute-start | bytes 294920 | tf_op jit(solution)/shard_map/ppermute | solution.py:19
  301.9 1.9 collective-permute-start.5
  303.9 1.3 fusion.133
  305.2 2.9 reshape.648
  308.4 2.0 fusion.9
  310.5 3.1 fusion.131
  313.5 7.9 %fusion.130 = (bf16[4,8,64,192]{3,2,1,0:T(8,128)(2,1)S(1)}, bf16[4,8,64,192]{3,2,1,0:T(8,128)(2,1)S(1)}, bf16[4,8,64,192]{3,2,1,0:T(8,128)(2,1)S(1)}, bf16[4,8,6...) fusion(bf16[6,10,66,192]{3,2,1,0:T(8,128)(2,1)S(1)} %fusion.9), kind=kLoop, calls=%fused_computation.271 | loop fusion | bytes 29884416 | tf_op jit(solution)/shard_map/slice | solution.py:45
  (594 shorter events, 150.1 us)
Async XLA Ops:
  6.5 1.4 copy-start
  6.5 137.6 %copy-start.91 = (bf16[3,27,96]{2,1,0:T(8,128)(2,1)S(1)}, bf16[3,27,96]{2,1,0:T(8,128)(2,1)}, u32[]{:S(2)}) copy-start(bf16[3,27,96]{2,1,0:T(8,128)(2,1)} %param.16) | copy-start | bytes 46660
  6.5 206.9 %all-gather.2.cloned.1.call-start = ((), (), s32[]{:S(2)}) async-start(), calls=%async_computation.1 | async-start | bytes 6389760 | tf_op jit(solution)/shard_map/all_gather | solution.py:97
  107.8 73.9 %copy-start.69 = (bf16[16,27,384]{2,0,1:T(8,128)(2,1)S(1)}, bf16[16,27,384]{2,0,1:T(8,128)(2,1)}, u32[]{:S(2)}) copy-start(bf16[16,27,384]{2,0,1:T(8,128)(2,1)} %param.14) | copy-start | bytes 995332
  107.8 28.1 %all-to-all-start = ((bf16[64,2,128]{2,1,0:T(2,128)(2,1)}), bf16[64,2,128]{2,1,0:T(2,128)(2,1)S(1)}, u32[]{:S(2)}, u32[]{:S(2)}) async-start(bf16[64,2,128]{2,1,0:T(2,128)(2,1)} %reshape.702), calls=%async_computation | async-start | bytes 65536 | tf_op jit(solution)/shard_map/all_to_all | solution.py:81
  137.1 44.4 %collective-permute-start = (bf16[4,1,16,16]{3,2,1,0:T(8,128)(2,1)S(1)}, bf16[4,1,16,16]{3,2,1,0:T(8,128)(2,1)S(1)}, u32[]{:S(2)}, u32[]{:S(2)}) collective-permute-start(bf16[4,1,16,16]{3,2,1,0:T(8,128)(2,1)S(1)} %get-tuple-element.157), channel_id=1, source_target_pairs={{0,1},{1,2},{2,3},{3,4},{4,5},{5,6},{6,7},{8,9},{9,10},{10,11},{11... | collective-permute-start | bytes 6152 | tf_op jit(solution)/shard_map/ppermute | solution.py:19
  142.2 39.3 %collective-permute-start.1 = (bf16[4,1,16,16]{3,2,1,0:T(8,128)(2,1)S(1)}, bf16[4,1,16,16]{3,2,1,0:T(8,128)(2,1)S(1)}, u32[]{:S(2)}, u32[]{:S(2)}) collective-permute-start(bf16[4,1,16,16]{3,2,1,0:T(8,128)(2,1)S(1)} %get-tuple-element.158), channel_id=1, source_target_pairs={{1,0},{2,1},{3,2},{4,3},{5,4},{6,5},{7,6},{9,8},{10,9},{11,10},{12... | collective-permute-start | bytes 6152 | tf_op jit(solution)/shard_map/ppermute | solution.py:21
  184.4 1.6 copy-start.92
  186.6 20.8 %collective-permute-start.2 = (bf16[4,1,32,384]{3,2,1,0:T(8,128)(2,1)S(1)}, bf16[4,1,32,384]{3,2,1,0:T(8,128)(2,1)S(1)}, u32[]{:S(2)}, u32[]{:S(2)}) collective-permute-start(bf16[4,1,32,384]{3,2,1,0:T(8,128)(2,1)S(1)} %get-tuple-element.129), channel_id=1, source_target_pairs={{0,1},{1,2},{2,3},{3,4},{4,5},{5,6},{6,7},{8,9},{9,10},{10,11},{11... | collective-permute-start | bytes 294920 | tf_op jit(solution)/shard_map/ppermute | solution.py:19
  201.2 6.2 %collective-permute-start.3 = (bf16[4,1,32,384]{3,2,1,0:T(8,128)(2,1)S(1)}, bf16[4,1,32,384]{3,2,1,0:T(8,128)(2,1)S(1)}, u32[]{:S(2)}, u32[]{:S(2)}) collective-permute-start(bf16[4,1,32,384]{3,2,1,0:T(8,128)(2,1)S(1)} %get-tuple-element.130), channel_id=1, source_target_pairs={{1,0},{2,1},{3,2},{4,3},{5,4},{6,5},{7,6},{9,8},{10,9},{11,10},{12... | collective-permute-start | bytes 294920 | tf_op jit(solution)/shard_map/ppermute | solution.py:21
  268.7 12.1 %copy-start.22 = (bf16[4,4,32,384]{3,2,1,0:T(8,128)(2,1)S(1)}, bf16[4,4,32,384]{3,2,1,0:T(8,128)(2,1)}, u32[]{:S(2)}) copy-start(bf16[4,4,32,384]{3,2,1,0:T(8,128)(2,1)} %get-tuple-element.121) | copy-start | bytes 1179652
  271.7 10.3 %copy-start.21 = (bf16[4,4,32,384]{3,2,1,0:T(8,128)(2,1)S(1)}, bf16[4,4,32,384]{3,2,1,0:T(8,128)(2,1)}, u32[]{:S(2)}) copy-start(bf16[4,4,32,384]{3,2,1,0:T(8,128)(2,1)} %get-tuple-element.122) | copy-start | bytes 1179652
  272.9 10.5 %copy-start.23 = (bf16[4,4,32,384]{3,2,1,0:T(8,128)(2,1)S(1)}, bf16[4,4,32,384]{3,2,1,0:T(8,128)(2,1)}, u32[]{:S(2)}) copy-start(bf16[4,4,32,384]{3,2,1,0:T(8,128)(2,1)} %get-tuple-element.102) | copy-start | bytes 1179652
  279.4 5.5 %copy-start.43 = (bf16[4,4,32,384]{3,2,1,0:T(8,128)(2,1)S(1)}, bf16[4,4,32,384]{3,2,1,0:T(8,128)(2,1)}, u32[]{:S(2)}) copy-start(bf16[4,4,32,384]{3,2,1,0:T(8,128)(2,1)} %get-tuple-element.119) | copy-start | bytes 1179652
  280.7 3.8 %copy-start.44 = (bf16[4,4,32,384]{3,2,1,0:T(8,128)(2,1)S(1)}, bf16[4,4,32,384]{3,2,1,0:T(8,128)(2,1)}, u32[]{:S(2)}) copy-start(bf16[4,4,32,384]{3,2,1,0:T(8,128)(2,1)} %get-tuple-element.120) | copy-start | bytes 1179652
  280.7 3.8 %copy-start.61 = (bf16[384,1,192]{0,2,1:T(8,128)(2,1)S(1)}, bf16[384,1,192]{0,2,1:T(8,128)(2,1)}, u32[]{:S(2)}) copy-start(bf16[384,1,192]{0,2,1:T(8,128)(2,1)} %copy.130) | copy-start | bytes 442372
  280.8 4.2 %copy-start.59 = (bf16[384,1,192]{0,2,1:T(8,128)(2,1)S(1)}, bf16[384,1,192]{0,2,1:T(8,128)(2,1)}, u32[]{:S(2)}) copy-start(bf16[384,1,192]{0,2,1:T(8,128)(2,1)} %copy.131) | copy-start | bytes 442372
  282.1 3.2 copy-start.42
  282.1 3.2 copy-start.57
  286.3 1.1 copy-start.66
  287.7 1.1 copy-start.62
  288.8 1.1 copy-start.56
  289.2 1.1 copy-start.54
  290.2 1.1 copy-start.49
  295.5 9.6 %copy-start.94 = (f32[96]{0:T(128)S(1)}, f32[96]{0:T(128)}, u32[]{:S(2)}) copy-start(f32[96]{0:T(128)} %param.19) | copy-start | bytes 1156
  298.3 9.8 %collective-permute-start.4 = (bf16[4,1,64,192]{3,2,1,0:T(8,128)(2,1)}, bf16[4,1,64,192]{3,2,1,0:T(8,128)(2,1)S(1)}, u32[]{:S(2)}, u32[]{:S(2)}) collective-permute-start(bf16[4,1,64,192]{3,2,1,0:T(8,128)(2,1)} %get-tuple-element.125), channel_id=1, source_target_pairs={{0,1},{1,2},{2,3},{3,4},{4,5},{5,6},{6,7},{8,9},{9,10},{10,11},{11... | collective-permute-start | bytes 294920 | tf_op jit(solution)/shard_map/ppermute | solution.py:19
  301.9 6.5 %collective-permute-start.5 = (bf16[4,1,64,192]{3,2,1,0:T(8,128)(2,1)}, bf16[4,1,64,192]{3,2,1,0:T(8,128)(2,1)S(1)}, u32[]{:S(2)}, u32[]{:S(2)}) collective-permute-start(bf16[4,1,64,192]{3,2,1,0:T(8,128)(2,1)} %get-tuple-element.126), channel_id=1, source_target_pairs={{1,0},{2,1},{3,2},{4,3},{5,4},{6,5},{7,6},{9,8},{10,9},{11,10},{12... | collective-permute-start | bytes 294920 | tf_op jit(solution)/shard_map/ppermute | solution.py:21
  321.9 1.2 copy-start.16
  321.9 1.2 copy-start.74
  322.4 1.3 copy-start.15
  322.4 1.3 copy-start.73
  323.2 1.3 copy-start.14
  323.7 1.3 copy-start.13
  324.5 1.3 copy-start.12
  325.0 1.3 copy-start.11
  325.8 1.3 copy-start.10
  326.3 1.4 copy-start.9
  327.3 1.4 copy-start.8
  328.3 1.4 copy-start.7
  329.2 1.4 copy-start.6
  330.2 1.4 copy-start.5
  331.2 1.4 copy-start.4
  332.2 1.4 copy-start.3
  333.1 1.4 copy-start.2
  339.1 1.2 copy-start.17
  339.1 1.2 copy-start.77
  339.6 1.2 copy-start.76
  343.3 2.0 copy-start.1
  (55 other events, 57.8 us)
Sparse Core Ops, SparseCore 0:
  10.3 95.0 all-gather.1
where the time goes:
time: 359 us; the launch traced here: 352 us
  local copies, waits for them, and re-layouts  208 us (58%)
  starting transfers between devices  46.8 us (13%)
  blocking collectives  37.3 us (10%)
  matrix products  27.2 us (8%)
  between operations  18.1 us (5%)
  other arithmetic  9.07 us (3%)
  waiting for transfers between devices  5.1 us (1%)
    gather x256, local copies, waits for them, and re-layouts  94.3 us
    unnamed x219, local copies, waits for them, and re-layouts  51.6 us
    all_gather x1, blocking collectives, per_device(): lax.all_gather(w_out, 'grp', axis=0, tiled=True)  37.3 us
    slice x4, local copies, waits for them, and re-layouts, causal_conv(): weight[:, tap_index, :]  29.1 us
    dot_general x81, matrix products, causal_conv(): jnp.dot(window, weight[:, tap_index, :], preferred_element_type=jnp.float32)  27.2 us
    ppermute x3, starting transfers between devices, extended_2(): lax.ppermute(tail, axis, [(i, (i + 1) % count) for i in range(ends)])  23.3 us
    all_to_all x1, starting transfers between devices, per_device(): lax.all_to_all(outgoing, 'grp', split_axis=0, concat_axis=0, tiled=True)  17.2 us
    slice x6, local copies, waits for them, and re-layouts, causal_conv(): padded[time_tap:time_tap + count_t, row_tap:row_tap + count_r, col_tap:co...  15.8 us
  transfers between devices with their start and end apart: 8, of which 2 were waited for; matrix products, arithmetic and copies ran while one was open for 35% of the time, Pallas kernels for 0%

commit v1 on v0

--- a/solution.py
+++ b/solution.py
@@ -95,7 +95,9 @@
     latent_in = jnp.where(valid, tokens, jnp.zeros((), tokens.dtype))
     full_mid, full_out = (
         lax.all_gather(w_mid, "grp", axis=0, tiled=True),
-        lax.all_gather(w_out, "grp", axis=0, tiled=True),
+        jnp.concatenate(
+            lax.all_to_all(jnp.stack([w_out] * lax.axis_size("grp")), "grp", 0, 0), axis=0
+        ),
     )
     latent_ext = extended_2(latent_in, (("row", 1),), 1)
     act_in = rms_silu(causal_conv(latent_ext, w_in), gain_in).astype(jnp.bfloat16)

time: 359 us -> 388 us (1.081)
  waiting for transfers between devices: 5.1 us -> 84.1 us
  blocking collectives: 37.3 us -> 0 us
  local copies, waits for them, and re-layouts: 208 us -> 198 us
    all_gather x1, waiting for transfers between devices: 0.02 us -> 56.3 us  [per_device(): lax.all_gather(w_mid, 'grp', axis=0, tiled=True)]
    all_gather x1 -> x0, blocking collectives: 37.3 us -> none  [per_device(): lax.all_gather(w_out, 'grp', axis=0, tiled=True)]
    all_to_all x0 -> x1, waiting for transfers between devices: none -> 20.4 us  [per_device(): lax.all_to_all(jnp.stack([w_out] * lax.axis_size('grp')), 'grp', 0, 0)]
    gather x256, local copies, waits for them, and re-layouts: 94.3 us -> 82.2 us
    ppermute x3, starting transfers between devices: 23.3 us -> 13.9 us  [extended_2(): lax.ppermute(tail, axis, [(i, (i + 1) % count) for i in range(ends)])]
    all_to_all x0 -> x1, starting transfers between devices: none -> 6.72 us  [per_device(): lax.all_to_all(jnp.stack([w_out] * lax.axis_size('grp')), 'grp', 0, 0)]
    unnamed x219 -> x221, local copies, waits for them, and re-layouts: 51.6 us -> 51.4 us
  transfers between devices with their start and end apart: 8 -> 9, of which waited for: 2 -> 5; matrix products, arithmetic and copies ran while one was open for 35% -> 6% of each run, Pallas kernels for 0% -> 0%
where the time goes in v1:
time: 388 us; the launch traced here: 381 us
  local copies, waits for them, and re-layouts  198 us (51%)
  waiting for transfers between devices  84.1 us (22%)
  starting transfers between devices  44 us (11%)
  matrix products  27.2 us (7%)
  between operations  17.6 us (5%)
  other arithmetic  8.91 us (2%)
    gather x256, local copies, waits for them, and re-layouts  82.2 us
    all_gather x1, waiting for transfers between devices, per_device(): lax.all_gather(w_mid, 'grp', axis=0, tiled=True)  56.3 us
    unnamed x221, local copies, waits for them, and re-layouts  51.4 us
    slice x4, local copies, waits for them, and re-layouts, causal_conv(): weight[:, tap_index, :]  29.6 us
    dot_general x81, matrix products, causal_conv(): jnp.dot(window, weight[:, tap_index, :], preferred_element_type=jnp.float32)  27.2 us
    all_to_all x1, waiting for transfers between devices, per_device(): lax.all_to_all(jnp.stack([w_out] * lax.axis_size('grp')), 'grp', 0, 0)  20.4 us
    all_to_all x1, starting transfers between devices, per_device(): lax.all_to_all(outgoing, 'grp', split_axis=0, concat_axis=0, tiled=True)  17.1 us
    slice x6, local copies, waits for them, and re-layouts, causal_conv(): padded[time_tap:time_tap + count_t, row_tap:row_tap + count_r, col_tap:co...  15.8 us
  transfers between devices with their start and end apart: 9, of which 5 were waited for; matrix products, arithmetic and copies ran while one was open for 6% of the time, Pallas kernels for 0%

profile of v1, /device:TPU:1, one launch (start us, length us, event | category | flops | bytes accessed | tf_op | source)
XLA Modules:
  0.0 380.7 jit_solution(7064072621599672120)
XLA Ops:
  8.0 1.4 gather_fusion
  10.5 82.7 %while.1 = (s32[]{:T(128)}, bf16[16384]{0:T(1024)(128)(2,1)S(1)}, s32[64,1]{0,1:T(1,128)S(1)}, bf16[64,256]{1,0:T(8,128)(2,1)S(1)}, s32[]{:T(128)}, /*index=5*/s32[]{:T(128)}) while((s32[]{:T(128)}, bf16[16384]{0:T(1024)(128)(2,1)S(1)}, s32[64,1]{0,1:T(1,128)S(1)}, bf16[64,256]{1,0:T(8,128)(2,1)S(1)}, s32[]{:T(128)}, /*index=5*/s32[]{:T(128)}) %tuple.141), condition=%wide.while_cond, body=%wide.while_body.sunk | while | flops 2 | bytes 3169 | solution.py:76
  95.1 17.1 %all-to-all-start = ((bf16[64,2,128]{2,1,0:T(2,128)(2,1)}), bf16[64,2,128]{2,1,0:T(2,128)(2,1)S(1)}, u32[]{:S(2)}, u32[]{:S(2)}) async-start(bf16[64,2,128]{2,1,0:T(2,128)(2,1)} %reshape.708), calls=%async_computation | async-start | bytes 65536 | tf_op jit(solution)/shard_map/all_to_all | solution.py:81
  115.2 1.2 dynamic_slice.7
  118.3 4.7 %all-to-all-done = bf16[64,2,128]{2,1,0:T(2,128)(2,1)S(1)} async-done(((bf16[64,2,128]{2,1,0:T(2,128)(2,1)}), bf16[64,2,128]{2,1,0:T(2,128)(2,1)S(1)}, u32[]{:S(2)}, u32[]{:S(2)}) %all-to-all-start) | async-done | bytes 32800 | tf_op jit(solution)/shard_map/all_to_all | solution.py:81
  124.2 5.1 %collective-permute-start = (bf16[4,1,16,16]{3,2,1,0:T(8,128)(2,1)S(1)}, bf16[4,1,16,16]{3,2,1,0:T(8,128)(2,1)S(1)}, u32[]{:S(2)}, u32[]{:S(2)}) collective-permute-start(bf16[4,1,16,16]{3,2,1,0:T(8,128)(2,1)S(1)} %get-tuple-element.157), channel_id=1, source_target_pairs={{0,1},{1,2},{2,3},{3,4},{4,5},{5,6},{6,7},{8,9},{9,10},{10,11},{11... | collective-permute-start | bytes 6152 | tf_op jit(solution)/shard_map/ppermute | solution.py:19
  129.3 1.9 collective-permute-start.1
  131.3 1.4 stack.2
  132.7 6.7 %all-to-all-start.1 = ((bf16[64,3,27,96]{3,2,1,0:T(8,128)(2,1)}), bf16[64,3,27,96]{3,2,1,0:T(8,128)(2,1)S(1)}, u32[]{:S(2)}, u32[]{:S(2)}) async-start(bf16[64,3,27,96]{3,2,1,0:T(8,128)(2,1)} %stack.2), calls=%async_computation.1 | async-start | bytes 3145728 | tf_op jit(solution)/shard_map/all_to_all | solution.py:99
  144.6 3.9 %collective-permute-start.2 = (bf16[4,1,32,384]{3,2,1,0:T(8,128)(2,1)S(1)}, bf16[4,1,32,384]{3,2,1,0:T(8,128)(2,1)S(1)}, u32[]{:S(2)}, u32[]{:S(2)}) collective-permute-start(bf16[4,1,32,384]{3,2,1,0:T(8,128)(2,1)S(1)} %get-tuple-element.129), channel_id=1, source_target_pairs={{0,1},{1,2},{2,3},{3,4},{4,5},{5,6},{6,7},{8,9},{9,10},{10,11},{11... | collective-permute-start | bytes 294920 | tf_op jit(solution)/shard_map/ppermute | solution.py:19
  148.6 2.4 collective-permute-start.3
  152.6 2.3 collective-permute-done.3
  156.2 1.4 fusion.189
  157.6 3.3 fusion.188
  160.9 20.4 %all-to-all-done.1 = bf16[64,3,27,96]{3,2,1,0:T(8,128)(2,1)S(1)} async-done(((bf16[64,3,27,96]{3,2,1,0:T(8,128)(2,1)}), bf16[64,3,27,96]{3,2,1,0:T(8,128)(2,1)S(1)}, u32[]{:S(2)}, u32[]{:S(2)}) %all-to-all-start.1) | async-done | bytes 995360 | tf_op jit(solution)/shard_map/all_to_all | solution.py:99
  181.3 2.7 fusion.186
  184.0 56.3 %all-gather.2.cloned.1.call-done = bf16[384,27,192]{2,1,0:T(8,128)(2,1)} async-done(((bf16[6,27,192]{2,1,0:T(8,128)(2,1)}), bf16[384,27,192]{2,1,0:T(8,128)(2,1)}) %all-gather.2.cloned.1.call-update) | async-done | bytes 3981328 | tf_op jit(solution)/shard_map/all_gather | solution.py:97
  240.3 8.7 %fusion.183 = (bf16[384,1,192]{2,1,0:T(2,128)(2,1)}, bf16[384,1,192]{2,1,0:T(2,128)(2,1)}, bf16[384,1,192]{2,1,0:T(2,128)(2,1)}, bf16[384,1,192]{2,1,0:T(2,128)(...) fusion(bf16[384,27,192]{2,1,0:T(8,128)(2,1)} %all-gather.2.clon, ...), kind=kLoop, calls=%fused_computation.297 | loop fusion | bytes 2359296 | tf_op jit(solution)/shard_map/slice | solution.py:53
  249.0 1.8 copy.111
  250.8 1.8 copy.110
  252.6 1.8 copy.109
  260.2 16.7 %fusion.182 = (bf16[384,1,192]{2,1,0:T(2,128)(2,1)}, bf16[384,1,192]{2,1,0:T(2,128)(2,1)}, bf16[384,1,192]{2,1,0:T(2,128)(2,1)}, bf16[384,1,192]{2,1,0:T(2,128)(...) fusion(bf16[384,27,192]{2,1,0:T(8,128)(2,1)} %all-gather.2.clon, ...), kind=kLoop, calls=%fused_computation.296 | loop fusion | bytes 5603328 | tf_op jit(solution)/shard_map/slice | solution.py:53
  276.9 1.8 copy.130
  278.7 1.8 copy.129
  280.5 1.8 copy.128
  282.3 1.8 copy.127
  284.1 1.8 copy.126
  285.9 1.8 copy.125
  287.7 1.8 copy.124
  289.5 1.8 copy.123
  291.3 1.8 copy.122
  293.1 1.8 copy.121
  296.0 1.9 copy.119
  300.2 1.8 copy.116
  302.0 1.8 copy.115
  303.8 1.8 copy.114
  306.8 1.3 copy.112
  308.1 1.3 fusion.64
  309.4 1.3 fusion.36
  321.1 1.8 broadcast_in_dim.66
  322.9 2.1 reshape.630
  325.6 4.8 %collective-permute-start.4 = (bf16[4,1,64,192]{3,2,1,0:T(8,128)(2,1)}, bf16[4,1,64,192]{3,2,1,0:T(8,128)(2,1)S(1)}, u32[]{:S(2)}, u32[]{:S(2)}) collective-permute-start(bf16[4,1,64,192]{3,2,1,0:T(8,128)(2,1)} %get-tuple-element.125), channel_id=1, source_target_pairs={{0,1},{1,2},{2,3},{3,4},{4,5},{5,6},{6,7},{8,9},{9,10},{10,11},{11... | collective-permute-start | bytes 294920 | tf_op jit(solution)/shard_map/ppermute | solution.py:19
  330.5 1.9 collective-permute-start.5
  332.4 1.4 fusion.187
  333.8 2.8 reshape.654
  337.0 2.0 fusion.9
  339.0 3.1 fusion.185
  342.1 7.9 %fusion.184 = (bf16[4,8,64,192]{3,2,1,0:T(8,128)(2,1)S(1)}, bf16[4,8,64,192]{3,2,1,0:T(8,128)(2,1)S(1)}, bf16[4,8,64,192]{3,2,1,0:T(8,128)(2,1)S(1)}, bf16[4,8,6...) fusion(bf16[6,10,66,192]{3,2,1,0:T(8,128)(2,1)S(1)} %fusion.9), kind=kLoop, calls=%fused_computation.298 | loop fusion | bytes 29884416 | tf_op jit(solution)/shard_map/slice | solution.py:45
  (598 shorter events, 142.4 us)
Async XLA Ops:
  6.5 124.8 %copy-start.92 = (bf16[3,27,96]{2,1,0:T(8,128)(2,1)S(1)}, bf16[3,27,96]{2,1,0:T(8,128)(2,1)}, u32[]{:S(2)}) copy-start(bf16[3,27,96]{2,1,0:T(8,128)(2,1)} %param.16) | copy-start | bytes 46660
  95.1 27.9 %all-to-all-start = ((bf16[64,2,128]{2,1,0:T(2,128)(2,1)}), bf16[64,2,128]{2,1,0:T(2,128)(2,1)S(1)}, u32[]{:S(2)}, u32[]{:S(2)}) async-start(bf16[64,2,128]{2,1,0:T(2,128)(2,1)} %reshape.708), calls=%async_computation | async-start | bytes 65536 | tf_op jit(solution)/shard_map/all_to_all | solution.py:81
  112.2 128.1 %all-gather.2.cloned.1.call-start = ((), (), s32[]{:S(2)}) async-start(), calls=%async_computation.2 | async-start | bytes 6389760 | tf_op jit(solution)/shard_map/all_gather | solution.py:97
  124.2 15.3 %collective-permute-start = (bf16[4,1,16,16]{3,2,1,0:T(8,128)(2,1)S(1)}, bf16[4,1,16,16]{3,2,1,0:T(8,128)(2,1)S(1)}, u32[]{:S(2)}, u32[]{:S(2)}) collective-permute-start(bf16[4,1,16,16]{3,2,1,0:T(8,128)(2,1)S(1)} %get-tuple-element.157), channel_id=1, source_target_pairs={{0,1},{1,2},{2,3},{3,4},{4,5},{5,6},{6,7},{8,9},{9,10},{10,11},{11... | collective-permute-start | bytes 6152 | tf_op jit(solution)/shard_map/ppermute | solution.py:19
  129.3 10.2 %collective-permute-start.1 = (bf16[4,1,16,16]{3,2,1,0:T(8,128)(2,1)S(1)}, bf16[4,1,16,16]{3,2,1,0:T(8,128)(2,1)S(1)}, u32[]{:S(2)}, u32[]{:S(2)}) collective-permute-start(bf16[4,1,16,16]{3,2,1,0:T(8,128)(2,1)S(1)} %get-tuple-element.158), channel_id=1, source_target_pairs={{1,0},{2,1},{3,2},{4,3},{5,4},{6,5},{7,6},{9,8},{10,9},{11,10},{12... | collective-permute-start | bytes 6152 | tf_op jit(solution)/shard_map/ppermute | solution.py:21
  132.7 6.9 %copy-start.69 = (bf16[16,27,384]{2,0,1:T(8,128)(2,1)S(1)}, bf16[16,27,384]{2,0,1:T(8,128)(2,1)}, u32[]{:S(2)}) copy-start(bf16[16,27,384]{2,0,1:T(8,128)(2,1)} %param.14) | copy-start | bytes 995332
  132.7 48.5 %all-to-all-start.1 = ((bf16[64,3,27,96]{3,2,1,0:T(8,128)(2,1)}), bf16[64,3,27,96]{3,2,1,0:T(8,128)(2,1)S(1)}, u32[]{:S(2)}, u32[]{:S(2)}) async-start(bf16[64,3,27,96]{3,2,1,0:T(8,128)(2,1)} %stack.2), calls=%async_computation.1 | async-start | bytes 3145728 | tf_op jit(solution)/shard_map/all_to_all | solution.py:99
  142.5 1.6 copy-start.93
  143.2 7.7 %copy-start.95 = (f32[96]{0:T(128)S(1)}, f32[96]{0:T(128)}, u32[]{:S(2)}) copy-start(f32[96]{0:T(128)} %param.19) | copy-start | bytes 1156
  144.6 7.9 %collective-permute-start.2 = (bf16[4,1,32,384]{3,2,1,0:T(8,128)(2,1)S(1)}, bf16[4,1,32,384]{3,2,1,0:T(8,128)(2,1)S(1)}, u32[]{:S(2)}, u32[]{:S(2)}) collective-permute-start(bf16[4,1,32,384]{3,2,1,0:T(8,128)(2,1)S(1)} %get-tuple-element.129), channel_id=1, source_target_pairs={{0,1},{1,2},{2,3},{3,4},{4,5},{5,6},{6,7},{8,9},{9,10},{10,11},{11... | collective-permute-start | bytes 294920 | tf_op jit(solution)/shard_map/ppermute | solution.py:19
  148.6 6.3 %collective-permute-start.3 = (bf16[4,1,32,384]{3,2,1,0:T(8,128)(2,1)S(1)}, bf16[4,1,32,384]{3,2,1,0:T(8,128)(2,1)S(1)}, u32[]{:S(2)}, u32[]{:S(2)}) collective-permute-start(bf16[4,1,32,384]{3,2,1,0:T(8,128)(2,1)S(1)} %get-tuple-element.130), channel_id=1, source_target_pairs={{1,0},{2,1},{3,2},{4,3},{5,4},{6,5},{7,6},{9,8},{10,9},{11,10},{12... | collective-permute-start | bytes 294920 | tf_op jit(solution)/shard_map/ppermute | solution.py:21
  296.0 12.1 %copy-start.22 = (bf16[4,4,32,384]{3,2,1,0:T(8,128)(2,1)S(1)}, bf16[4,4,32,384]{3,2,1,0:T(8,128)(2,1)}, u32[]{:S(2)}) copy-start(bf16[4,4,32,384]{3,2,1,0:T(8,128)(2,1)} %get-tuple-element.121) | copy-start | bytes 1179652
  299.0 10.4 %copy-start.21 = (bf16[4,4,32,384]{3,2,1,0:T(8,128)(2,1)S(1)}, bf16[4,4,32,384]{3,2,1,0:T(8,128)(2,1)}, u32[]{:S(2)}) copy-start(bf16[4,4,32,384]{3,2,1,0:T(8,128)(2,1)} %get-tuple-element.122) | copy-start | bytes 1179652
  300.2 10.5 %copy-start.23 = (bf16[4,4,32,384]{3,2,1,0:T(8,128)(2,1)S(1)}, bf16[4,4,32,384]{3,2,1,0:T(8,128)(2,1)}, u32[]{:S(2)}) copy-start(bf16[4,4,32,384]{3,2,1,0:T(8,128)(2,1)} %get-tuple-element.102) | copy-start | bytes 1179652
  306.8 5.5 %copy-start.43 = (bf16[4,4,32,384]{3,2,1,0:T(8,128)(2,1)S(1)}, bf16[4,4,32,384]{3,2,1,0:T(8,128)(2,1)}, u32[]{:S(2)}) copy-start(bf16[4,4,32,384]{3,2,1,0:T(8,128)(2,1)} %get-tuple-element.119) | copy-start | bytes 1179652
  308.1 3.8 %copy-start.44 = (bf16[4,4,32,384]{3,2,1,0:T(8,128)(2,1)S(1)}, bf16[4,4,32,384]{3,2,1,0:T(8,128)(2,1)}, u32[]{:S(2)}) copy-start(bf16[4,4,32,384]{3,2,1,0:T(8,128)(2,1)} %get-tuple-element.120) | copy-start | bytes 1179652
  308.1 3.8 %copy-start.61 = (bf16[384,1,192]{0,2,1:T(8,128)(2,1)S(1)}, bf16[384,1,192]{0,2,1:T(8,128)(2,1)}, u32[]{:S(2)}) copy-start(bf16[384,1,192]{0,2,1:T(8,128)(2,1)} %copy.106) | copy-start | bytes 442372
  308.1 4.2 %copy-start.59 = (bf16[384,1,192]{0,2,1:T(8,128)(2,1)S(1)}, bf16[384,1,192]{0,2,1:T(8,128)(2,1)}, u32[]{:S(2)}) copy-start(bf16[384,1,192]{0,2,1:T(8,128)(2,1)} %copy.107) | copy-start | bytes 442372
  309.4 3.2 copy-start.42
  309.4 3.2 copy-start.57
  313.7 1.1 copy-start.66
  315.1 1.1 copy-start.62
  316.5 1.1 copy-start.54
  317.6 1.1 copy-start.49
  325.6 11.0 %collective-permute-start.4 = (bf16[4,1,64,192]{3,2,1,0:T(8,128)(2,1)}, bf16[4,1,64,192]{3,2,1,0:T(8,128)(2,1)S(1)}, u32[]{:S(2)}, u32[]{:S(2)}) collective-permute-start(bf16[4,1,64,192]{3,2,1,0:T(8,128)(2,1)} %get-tuple-element.125), channel_id=1, source_target_pairs={{0,1},{1,2},{2,3},{3,4},{4,5},{5,6},{6,7},{8,9},{9,10},{10,11},{11... | collective-permute-start | bytes 294920 | tf_op jit(solution)/shard_map/ppermute | solution.py:19
  330.5 6.5 %collective-permute-start.5 = (bf16[4,1,64,192]{3,2,1,0:T(8,128)(2,1)}, bf16[4,1,64,192]{3,2,1,0:T(8,128)(2,1)S(1)}, u32[]{:S(2)}, u32[]{:S(2)}) collective-permute-start(bf16[4,1,64,192]{3,2,1,0:T(8,128)(2,1)} %get-tuple-element.126), channel_id=1, source_target_pairs={{1,0},{2,1},{3,2},{4,3},{5,4},{6,5},{7,6},{9,8},{10,9},{11,10},{12... | collective-permute-start | bytes 294920 | tf_op jit(solution)/shard_map/ppermute | solution.py:21
  342.1 8.4 %copy-start.73 = (bf16[192,1,96]{2,1,0:T(2,128)(2,1)S(1)}, bf16[192,1,96]{2,1,0:T(2,128)(2,1)}, u32[]{:S(2)}) copy-start(bf16[192,1,96]{2,1,0:T(2,128)(2,1)} %get-tuple-element.73) | copy-start | bytes 110596
  350.5 1.2 copy-start.16
  350.5 1.2 copy-start.75
  351.0 1.3 copy-start.15
  351.0 1.3 copy-start.74
  351.7 1.3 copy-start.14
  352.3 1.3 copy-start.13
  353.0 1.3 copy-start.12
  353.6 1.3 copy-start.11
  354.3 1.3 copy-start.10
  354.9 1.3 copy-start.9
  355.7 1.4 copy-start.8
  356.6 1.4 copy-start.7
  357.6 1.4 copy-start.6
  358.6 1.4 copy-start.5
  359.5 1.4 copy-start.4
  360.5 1.4 copy-start.3
  361.5 1.4 copy-start.2
  367.5 1.2 copy-start.17
  367.5 1.2 copy-start.78
  367.9 1.2 copy-start.77
  371.7 2.0 copy-start.1
  (57 other events, 59.6 us)
Sparse Core Ops, SparseCore 0:
  131.4 108.8 all-gather.1
